TPU v7x, 32 devices: a whole 2x2x4 slice. The times are simulated.
32 devices in a mesh: group: 2 (over x), expert: 16 (over z, y, core).
Axes of the slice: x: 2, y: 2, z: 4, core: 2. Of those that a mesh axis runs over, the one named last changes fastest.
Arguments:
- tokens: bfloat16 [128, 7168], P(('group', 'expert')), parts along dimension 0, may hold values from -6 to 6
- expert_ids: int32 [128, 2], P(('group', 'expert')), parts along dimension 0, may hold values from 0 to 1, all different within a row; in each aligned block of 4 rows (0 to 3, 4 to 7, ...) at most 4 rows name the same one
- gate_codes: int32 [128, 2], P(('group', 'expert')), parts along dimension 0, may hold values from 1 to 65535
- gate_weight: bfloat16 [16, 7168, 256], P('expert'), may hold values from -0.0625 to 0.0625
- up_weight: bfloat16 [16, 7168, 256], P('expert'), may hold values from -0.0625 to 0.0625
- down_weight: bfloat16 [16, 256, 7168], P('expert'), may hold values from -0.125 to 0.125
- target_basis: bfloat16 [7168, 512], P('expert'), may hold values from -0.0625 to 0.0625
Outputs:
- targets: bfloat16 [128, 512], P(('group', 'expert')), parts along dimension 0
There are 2 independent parts, one for each index of `group`. A program takes and returns all parts, laid end to end along the dimension named above; an argument that names none is the same for every part. Nothing has to cross between parts.
Inputs may be any that keep to these rules, and one draw needn't show every extreme that they name: `expert_ids`: each row names 2 different experts; among the 4 rows of one device no expert is named more than 4 times, a bound that some block reaches.
All inputs are finite; a program needn't handle non-finite values.
Results may differ from a plain program's by a relative error of at most 0.0057.
Values may be sent and summed in bfloat16 or wider, within the bound.
No kernel may reach another device: no remote copies, remote signals or barrier semaphores. Data moves between devices by JAX's collectives and lax.ppermute only.
A program may use at most 128 MiB of HBM per device.

v0:
```python
import jax
import jax.numpy as jnp
from jax import lax
from jax.sharding import PartitionSpec as P

SLICES = 8


def run_expert(received, gate_weight, up_weight, down_weight):
    sources, slots, feature_width = received.shape
    row_block = received.reshape(sources * slots, feature_width)
    gate_act = jnp.dot(row_block, gate_weight[0], preferred_element_type=jnp.float32)
    up_act = jnp.dot(row_block, up_weight[0], preferred_element_type=jnp.float32)
    hidden = (jax.nn.silu(gate_act) * up_act).astype(jnp.bfloat16)
    expert_part = jnp.dot(hidden, down_weight[0], preferred_element_type=jnp.float32).astype(
        jnp.bfloat16
    )
    return expert_part.reshape(sources, slots, feature_width)


def shards(tokens, expert_ids, gate_codes, gate_weight, up_weight, down_weight, target_basis):
    token_count, feature_width = tokens.shape
    pick_count = expert_ids.shape[1]
    owner_count = lax.axis_size("expert")
    expert_count = owner_count // SLICES
    capacity = min(token_count, max(2, 5 * token_count * pick_count // (4 * expert_count)))
    rank_width = target_basis.shape[1]
    flat_ids = expert_ids.reshape(-1)
    onehot = (flat_ids[:, None] == jnp.arange(expert_count, dtype=jnp.int32)[None, :]).astype(
        jnp.int32
    )
    before = jnp.cumsum(onehot, axis=0) - onehot
    slot_rank = jnp.sum(before * onehot, axis=1)
    slot_index = flat_ids * capacity + slot_rank
    row_token = jnp.arange(token_count * pick_count, dtype=jnp.int32) // pick_count
    slot_table = (
        jnp.full((expert_count * capacity,), token_count, jnp.int32).at[slot_index].set(row_token)
    )
    padded = jnp.concatenate([tokens, jnp.zeros((1, feature_width), tokens.dtype)], axis=0)
    per_expert_rows = padded[slot_table].reshape(expert_count, 1, capacity, feature_width)
    outgoing = jnp.broadcast_to(per_expert_rows, (expert_count, SLICES, capacity, feature_width))
    outgoing = outgoing.reshape(owner_count, capacity, feature_width)
    full_basis = lax.all_gather(target_basis, "expert", axis=0, tiled=True)
    expert_part = run_expert(
        lax.all_to_all(outgoing, "expert", split_axis=0, concat_axis=0, tiled=True),
        gate_weight,
        up_weight,
        down_weight,
    )
    result = jnp.einsum("skd,dr->skr", expert_part, full_basis, preferred_element_type=jnp.float32)
    returned = lax.all_to_all(result, "expert", split_axis=0, concat_axis=0, tiled=True)
    summed = jnp.sum(returned.reshape(expert_count, SLICES, capacity, rank_width), axis=1)
    projected = summed.reshape(expert_count * capacity, rank_width)[slot_index]
    codes_float = gate_codes.astype(jnp.float32)
    weights = 2.5 * codes_float / jnp.sum(codes_float, axis=1, keepdims=True)
    projected = projected.reshape(token_count, pick_count, rank_width)
    return jnp.sum(weights[:, :, None] * projected, axis=1).astype(jnp.bfloat16)


def solution(mesh):
    in_specs = (
        P(("group", "expert"), None),
        P(("group", "expert"), None),
        P(("group", "expert"), None),
        P("expert", None, None),
        P("expert", None, None),
        P("expert", None, None),
        P("expert", None),
    )
    out_specs = P(("group", "expert"), None)
    return jax.shard_map(shards, mesh=mesh, in_specs=in_specs, out_specs=out_specs, check_vma=False)
```

profile of v0, /device:TPU:0, one launch (start us, length us, event | category | flops | bytes accessed | tf_op | source)
XLA Modules:
  0.0 121.8 jit_solution(8186890199680378276)
XLA Ops:
  6.5 0.7 all-gather.2.cloned.1.call-update
  7.3 0.8 copy.25
  8.1 0.7 broadcast_multiply_fusion
  8.8 0.1 copy.24
  8.9 0.1 mul.37
  9.0 0.2 reduce_window_sum.11
  9.2 0.8 concatenate.3
  10.1 0.6 scatter_custom_fusion
  10.7 0.6 gather_fusion
  11.4 1.2 broadcast_in_dim.8
  12.5 7.4 %all-to-all-start = ((bf16[16,4,7168]{2,1,0:T(4,128)(2,1)}), bf16[16,4,7168]{2,1,0:T(4,128)(2,1)S(1)}, u32[]{:S(2)}, u32[]{:S(2)}) async-start(bf16[16,4,7168]{2,1,0:T(4,128)(2,1)} %bitcast.2), calls=%async_computation | async-start | bytes 1835008 | tf_op jit(solution)/shard_map/all_to_all | solution.py:45
  20.0 35.1 %all-to-all-done = bf16[16,4,7168]{2,1,0:T(4,128)(2,1)S(1)} async-done(((bf16[16,4,7168]{2,1,0:T(4,128)(2,1)}), bf16[16,4,7168]{2,1,0:T(4,128)(2,1)S(1)}, u32[]{:S(2)}, u32[]{:S(2)}) %all-to-all-start) | async-done | bytes 917536 | tf_op jit(solution)/shard_map/all_to_all | solution.py:45
  55.1 0.2 reshape.53
  55.3 2.8 %fusion.5 = f32[64,256]{1,0:T(8,128)S(1)} fusion(bf16[64,7168]{1,0:T(8,128)(2,1)S(1)} %reshape.53, bf16[1,7168,256]{2,1,0:T(8,128)(2,1)} %param.10), kind=kOutput, calls=%fused_computation.9 | convolution fusion | flops 234881024 | bytes 4653056 | tf_op jit(solution)/shard_map/dot_general | solution.py:12
  58.0 5.5 %convolution_convert_fusion = bf16[64,7168]{1,0:T(8,128)(2,1)S(1)} fusion(bf16[1,256,7168]{2,1,0:T(8,128)(2,1)} %param.12, bf16[64,7168]{1,0:T(8,128)(2,1)S(1)} %reshape.53, bf16[1,7168,256]{2,1,0:T(8,128)(2,1)} %param.11, f32[64,256]{1,0:T(8,128)S(1)} %fusion.5), kind=kOutput, calls=%fused_computation.3 | convolution fusion | flops 470319104 | bytes 9240576 | tf_op jit(solution)/shard_map/dot_general | solution.py:15
  63.5 0.3 reshape.54
  63.8 33.4 %all-gather.2.cloned.1.call-done = bf16[7168,512]{1,0:T(8,128)(2,1)} async-done(((bf16[448,512]{1,0:T(8,128)(2,1)}), bf16[7168,512]{1,0:T(8,128)(2,1)}) %all-gather.2.cloned.1.call-update) | async-done | bytes 7340048 | tf_op jit(solution)/shard_map/all_gather | solution.py:43
  97.3 4.2 %fusion = f32[16,4,512]{2,0,1:T(8,128)S(1)} fusion(bf16[7168,512]{1,0:T(8,128)(2,1)} %all-gather.2.cloned.1.call-done, bf16[16,4,7168]{2,1,0:T(4,128)(2,1)S(1)} %reshape.54), kind=kOutput, calls=%fused_computation.4 | convolution fusion | flops 469762048 | bytes 8388608 | tf_op jit(solution)/shard_map/skd,dr->skr/dot_general | solution.py:50
  101.5 0.7 copy.27
  102.2 3.5 %all-to-all-start.1 = ((f32[16,4,512]{2,1,0:T(4,128)}), f32[16,4,512]{2,1,0:T(4,128)S(1)}, u32[]{:S(2)}, u32[]{:S(2)}) async-start(f32[16,4,512]{2,1,0:T(4,128)} %copy.27), calls=%async_computation.1 | async-start | bytes 262144 | tf_op jit(solution)/shard_map/all_to_all | solution.py:51
  105.8 0.1 copy.23
  105.9 7.8 %all-to-all-done.1 = f32[16,4,512]{2,1,0:T(4,128)S(1)} async-done(((f32[16,4,512]{2,1,0:T(4,128)}), f32[16,4,512]{2,1,0:T(4,128)S(1)}, u32[]{:S(2)}, u32[]{:S(2)}) %all-to-all-start.1) | async-done | bytes 131104 | tf_op jit(solution)/shard_map/all_to_all | solution.py:51
  113.7 0.6 gather_fusion.1
  114.2 0.7 multiply_reduce_fusion
  (17 shorter events, 0.3 us)
Async XLA Ops:
  6.5 13.4 %copy-start = (s32[4,2]{0,1:T(2,128)S(1)}, s32[4,2]{0,1:T(2,128)}, u32[]{:S(2)}) copy-start(s32[4,2]{0,1:T(2,128)} %param.9) | copy-start | bytes 100
  6.5 90.7 %all-gather.2.cloned.1.call-start = ((), (), s32[]{:S(2)}) async-start(), calls=%async_computation.2 | async-start | bytes 7798784 | tf_op jit(solution)/shard_map/all_gather | solution.py:43
  12.5 42.5 %all-to-all-start = ((bf16[16,4,7168]{2,1,0:T(4,128)(2,1)}), bf16[16,4,7168]{2,1,0:T(4,128)(2,1)S(1)}, u32[]{:S(2)}, u32[]{:S(2)}) async-start(bf16[16,4,7168]{2,1,0:T(4,128)(2,1)} %bitcast.2), calls=%async_computation | async-start | bytes 1835008 | tf_op jit(solution)/shard_map/all_to_all | solution.py:45
  102.2 11.4 %all-to-all-start.1 = ((f32[16,4,512]{2,1,0:T(4,128)}), f32[16,4,512]{2,1,0:T(4,128)S(1)}, u32[]{:S(2)}, u32[]{:S(2)}) async-start(f32[16,4,512]{2,1,0:T(4,128)} %copy.27), calls=%async_computation.1 | async-start | bytes 262144 | tf_op jit(solution)/shard_map/all_to_all | solution.py:51
Sparse Core Ops, SparseCore 0:
  9.6 87.5 all-gather.1
where the time goes:
time: 122 us
  waiting for transfers between devices  77 us (63%)
  between operations  13.5 us (11%)
  matrix products  12.4 us (10%)
  starting transfers between devices  10.9 us (9%)
  local copies, waits for them, and re-layouts  6.25 us (5%)
  other arithmetic  1.66 us (1%)
    all_to_all x1, waiting for transfers between devices, shards(): lax.all_to_all(outgoing, 'expert', split_axis=0, concat_axis=0, tiled=True)  35.1 us
    all_gather x1, waiting for transfers between devices, shards(): full_basis = lax.all_gather(target_basis, 'expert', axis=0, tiled=True)  33.4 us
    all_to_all x1, waiting for transfers between devices, shards(): lax.all_to_all(result, 'expert', split_axis=0, concat_axis=0, tiled=True)  7.76 us
    all_to_all x1, starting transfers between devices, shards(): lax.all_to_all(outgoing, 'expert', split_axis=0, concat_axis=0, tiled=True)  7.41 us
    dot_general x1, matrix products, run_expert(): jnp.dot(hidden, down_weight[0], preferred_element_type=jnp.float32)  5.45 us
    dot_general x1, matrix products, shards(): jnp.einsum('skd,dr->skr', expert_part, full_basis, preferred_element_type...  4.23 us
    all_to_all x1, starting transfers between devices, shards(): lax.all_to_all(result, 'expert', split_axis=0, concat_axis=0, tiled=True)  3.51 us
    dot_general x1, matrix products, run_expert(): jnp.dot(row_block, gate_weight[0], preferred_element_type=jnp.float32)  2.76 us
  transfers between devices with their start and end apart: 3, of which 3 were waited for; matrix products, arithmetic and copies ran while one was open for 12% of the time, Pallas kernels for 0%

commit v1 on v0

--- a/solution.py
+++ b/solution.py
@@ -40,7 +40,10 @@
     per_expert_rows = padded[slot_table].reshape(expert_count, 1, capacity, feature_width)
     outgoing = jnp.broadcast_to(per_expert_rows, (expert_count, SLICES, capacity, feature_width))
     outgoing = outgoing.reshape(owner_count, capacity, feature_width)
-    full_basis = lax.all_gather(target_basis, "expert", axis=0, tiled=True)
+    peers = lax.axis_size("expert")
+    blocks = jnp.stack([target_basis for _ in range(peers)])
+    blocks = lax.all_to_all(blocks, "expert", split_axis=0, concat_axis=0)
+    full_basis = jnp.concatenate(blocks, axis=0)
     expert_part = run_expert(
         lax.all_to_all(outgoing, "expert", split_axis=0, concat_axis=0, tiled=True),
         gate_weight,

time: 122 us -> 222 us (1.82)
  waiting for transfers between devices: 77 us -> 131 us
  blocking collectives: 0 us -> 29.6 us
  starting transfers between devices: 10.9 us -> 37.3 us
  between operations: 13.5 us -> 0.12 us
  local copies, waits for them, and re-layouts: 6.25 us -> 9.07 us
    all_to_all x1, waiting for transfers between devices: 35.1 us -> 123 us  [shards(): blocks = lax.all_to_all(blocks, 'expert', split_axis=0, concat_axis=0)]
    all_gather x1 -> x0, waiting for transfers between devices: 33.4 us -> none  [shards(): full_basis = lax.all_gather(target_basis, 'expert', axis=0, tiled=True)]
    all_to_all x0 -> x1, blocking collectives: none -> 29.6 us  [shards(): lax.all_to_all(outgoing, 'expert', split_axis=0, concat_axis=0, tiled=True)]
    all_to_all x1, starting transfers between devices: 3.51 us -> 32.5 us  [shards(): lax.all_to_all(result, 'expert', split_axis=0, concat_axis=0, tiled=True)]
    another operation x0 -> x1, local copies, waits for them, and re-layouts: none -> 3.74 us  [shards(): blocks = jnp.stack([target_basis for _ in range(peers)])]
    all_to_all x1, starting transfers between devices: 7.41 us -> 4.82 us  [shards(): blocks = lax.all_to_all(blocks, 'expert', split_axis=0, concat_axis=0)]
  transfers between devices with their start and end apart: 3 -> 2, of which waited for: 3 -> 2; matrix products, arithmetic and copies ran while one was open for 12% -> 4% of each run, Pallas kernels for 0% -> 0%
where the time goes in v1:
time: 222 us
  waiting for transfers between devices  131 us (59%)
  starting transfers between devices  37.3 us (17%)
  blocking collectives  29.6 us (13%)
  matrix products  12.4 us (6%)
  local copies, waits for them, and re-layouts  9.07 us (4%)
    all_to_all x1, waiting for transfers between devices, shards(): blocks = lax.all_to_all(blocks, 'expert', split_axis=0, concat_axis=0)  123 us
    all_to_all x1, starting transfers between devices, shards(): lax.all_to_all(result, 'expert', split_axis=0, concat_axis=0, tiled=True)  32.5 us
    all_to_all x1, blocking collectives, shards(): lax.all_to_all(outgoing, 'expert', split_axis=0, concat_axis=0, tiled=True)  29.6 us
    all_to_all x1, waiting for transfers between devices, shards(): lax.all_to_all(result, 'expert', split_axis=0, concat_axis=0, tiled=True)  7.79 us
    dot_general x1, matrix products, run_expert(): jnp.dot(hidden, down_weight[0], preferred_element_type=jnp.float32)  5.45 us
    all_to_all x1, starting transfers between devices, shards(): blocks = lax.all_to_all(blocks, 'expert', split_axis=0, concat_axis=0)  4.82 us
  transfers between devices with their start and end apart: 2, of which 2 were waited for; matrix products, arithmetic and copies ran while one was open for 4% of the time, Pallas kernels for 0%

profile of v1, /device:TPU:0, one launch (start us, length us, event | category | flops | bytes accessed | tf_op | source)
XLA Modules:
  0.0 221.5 jit_solution(3737642472663608270)
XLA Ops:
  0.0 0.7 broadcast_multiply_fusion
  0.7 0.8 copy.25
  1.5 0.1 copy.24
  1.6 0.1 mul.37
  1.8 0.2 reduce_window_sum.11
  2.0 0.6 scatter_custom_fusion
  2.6 0.8 concatenate.3
  3.5 0.6 gather_fusion
  4.2 0.2 broadcast_in_dim.8
  4.4 29.6 %all_to_all.15 = bf16[16,4,7168]{2,1,0:T(4,128)(2,1)S(1)} all-to-all(bf16[16,4,7168]{2,1,0:T(4,128)(2,1)S(1)} %bitcast.30), channel_id=1, replica_groups=mesh['group'=2,'expert'=16] {'expert'}, dimensions={0} | all-to-all | bytes 1835008 | tf_op jit(solution)/shard_map/all_to_all | solution.py:48
  34.0 3.7 %stack.2 = bf16[16,448,512]{2,1,0:T(8,128)(2,1)} broadcast(bf16[448,512]{1,0:T(8,128)(2,1)S(1)} %copy-done), dimensions={1,2} | broadcast | bytes 7798784 | tf_op jit(solution)/shard_map/stack | solution.py:44
  37.8 4.8 %all-to-all-start.1 = ((bf16[16,448,512]{2,1,0:T(8,128)(2,1)}), bf16[16,448,512]{2,1,0:T(8,128)(2,1)}, u32[]{:S(2)}, u32[]{:S(2)}) async-start(bf16[16,448,512]{2,1,0:T(8,128)(2,1)} %stack.2), calls=%async_computation.1 | async-start | bytes 14680064 | tf_op jit(solution)/shard_map/all_to_all | solution.py:45
  42.6 0.2 reshape.58
  42.8 2.8 %fusion.3 = f32[64,256]{1,0:T(8,128)S(1)} fusion(bf16[64,7168]{1,0:T(8,128)(2,1)S(1)} %reshape.58, bf16[1,7168,256]{2,1,0:T(8,128)(2,1)} %param.10), kind=kOutput, calls=%fused_computation.7 | convolution fusion | flops 234881024 | bytes 4653056 | tf_op jit(solution)/shard_map/dot_general | solution.py:12
  45.6 5.5 %convolution_convert_fusion = bf16[64,7168]{1,0:T(8,128)(2,1)S(1)} fusion(bf16[1,256,7168]{2,1,0:T(8,128)(2,1)} %param.12, bf16[64,7168]{1,0:T(8,128)(2,1)S(1)} %reshape.58, bf16[1,7168,256]{2,1,0:T(8,128)(2,1)} %param.11, f32[64,256]{1,0:T(8,128)S(1)} %fusion.3), kind=kOutput, calls=%fused_computation.3 | convolution fusion | flops 470319104 | bytes 9240576 | tf_op jit(solution)/shard_map/dot_general | solution.py:15
  51.0 0.3 reshape.59
  51.4 123.5 %all-to-all-done.1 = bf16[16,448,512]{2,1,0:T(8,128)(2,1)} async-done(((bf16[16,448,512]{2,1,0:T(8,128)(2,1)}), bf16[16,448,512]{2,1,0:T(8,128)(2,1)}, u32[]{:S(2)}, u32[]{:S(2)}) %all-to-all-start.1) | async-done | bytes 7340064 | tf_op jit(solution)/shard_map/all_to_all | solution.py:45
  174.8 4.2 %fusion.11 = f32[16,4,512]{2,0,1:T(8,128)S(1)} fusion(bf16[7168,512,1]{1,0,2:T(8,128)(2,1)} %bitcast.7, bf16[16,4,7168]{2,1,0:T(4,128)(2,1)S(1)} %reshape.59), kind=kOutput, calls=%fused_computation.11 | convolution fusion | flops 469762048 | bytes 8388608 | tf_op jit(solution)/shard_map/skd,dr->skr/dot_general | solution.py:53
  179.1 0.7 copy.27
  179.8 32.5 %all-to-all-start.2 = ((f32[16,4,512]{2,1,0:T(4,128)}), f32[16,4,512]{2,1,0:T(4,128)S(1)}, u32[]{:S(2)}, u32[]{:S(2)}) async-start(f32[16,4,512]{2,1,0:T(4,128)} %copy.27), calls=%async_computation.2 | async-start | bytes 262144 | tf_op jit(solution)/shard_map/all_to_all | solution.py:54
  212.3 0.1 copy.23
  212.4 7.8 %all-to-all-done.2 = f32[16,4,512]{2,1,0:T(4,128)S(1)} async-done(((f32[16,4,512]{2,1,0:T(4,128)}), f32[16,4,512]{2,1,0:T(4,128)S(1)}, u32[]{:S(2)}, u32[]{:S(2)}) %all-to-all-start.2) | async-done | bytes 131104 | tf_op jit(solution)/shard_map/all_to_all | solution.py:54
  220.2 0.6 gather_fusion.1
  220.8 0.7 multiply_reduce_fusion
  (18 shorter events, 0.3 us)
Async XLA Ops:
  0.0 34.0 %copy-start = (bf16[448,512]{1,0:T(8,128)(2,1)S(1)}, bf16[448,512]{1,0:T(8,128)(2,1)}, u32[]{:S(2)}) copy-start(bf16[448,512]{1,0:T(8,128)(2,1)} %param.13) | copy-start | bytes 1376260
  37.8 4.8 %copy-start.1 = (s32[4,2]{0,1:T(2,128)S(1)}, s32[4,2]{0,1:T(2,128)}, u32[]{:S(2)}) copy-start(s32[4,2]{0,1:T(2,128)} %param.9) | copy-start | bytes 100
  37.8 137.1 %all-to-all-start.1 = ((bf16[16,448,512]{2,1,0:T(8,128)(2,1)}), bf16[16,448,512]{2,1,0:T(8,128)(2,1)}, u32[]{:S(2)}, u32[]{:S(2)}) async-start(bf16[16,448,512]{2,1,0:T(8,128)(2,1)} %stack.2), calls=%async_computation.1 | async-start | bytes 14680064 | tf_op jit(solution)/shard_map/all_to_all | solution.py:45
  179.8 40.4 %all-to-all-start.2 = ((f32[16,4,512]{2,1,0:T(4,128)}), f32[16,4,512]{2,1,0:T(4,128)S(1)}, u32[]{:S(2)}, u32[]{:S(2)}) async-start(f32[16,4,512]{2,1,0:T(4,128)} %copy.27), calls=%async_computation.2 | async-start | bytes 262144 | tf_op jit(solution)/shard_map/all_to_all | solution.py:54
